TPU v7x, 32 devices: a whole 2x2x4 slice. The times are simulated.
32 devices in a mesh: expert: 8 (over z, y), dp: 4 (over x, core).
Axes of the slice: x: 2, y: 2, z: 4, core: 2. Of those that a mesh axis runs over, the one named last changes fastest.
Arguments:
- tokens_t: bfloat16 [7168, 512], P('expert', 'dp'), may hold values from -6 to 6
- slot_row: int32 [4, 1024], P('dp'), may hold values from -1 to 127, as said below
- slot_gate: float32 [4, 1024], P('dp'), may hold values from 0.2 to 1
- block_hot: int32 [4, 8], P('dp'), may hold values from 0 to 1, as said below
- hot_owner: int32 [1], replicated, may hold values from 0 to 255
- w_in: bfloat16 [4, 2, 2048, 7168], P('dp', None, 'expert'), may hold values from -0.0625 to 0.0625
- w_out: bfloat16 [4, 7168, 2048], P('dp', None, 'expert'), may hold values from -0.125 to 0.125
Outputs:
- mixed_t: bfloat16 [7168, 512], P('expert', 'dp')
Inputs may be any that keep to these rules, and one draw needn't show every extreme that they name: `slot_row`: each source shard fills each of its slots with a token of that shard or leaves it empty; a token may fill several slots. `block_hot`: every expert group runs at least one block of the hot expert and at least one block of its own expert.
All inputs are finite; a program needn't handle non-finite values.
Results may differ from a plain program's by a relative error of at most 0.014.
Values may be sent and summed in bfloat16 or wider, within the bound.
No kernel may reach another device: no remote copies, remote signals or barrier semaphores. Data moves between devices by JAX's collectives and lax.ppermute only.
A program may use at most 192 MiB of HBM per device.

v0:
```python
import jax
import jax.numpy as jnp
from jax import lax
from jax.sharding import PartitionSpec as P

BLOCK = 128


def from_root(value, axis, source):
    kept = jnp.where(lax.axis_index(axis) == source, value, 0).astype(value.dtype)
    return lax.psum(kept, axis)


def local(tokens_t, slot_row, slot_gate, block_hot, hot_owner, w_in, w_out):
    slot_ids = slot_row[0]
    slot_weights = slot_gate[0]
    hot_flags = block_hot[0]
    num_blocks = hot_flags.shape[0]
    tok_local = tokens_t.shape[1]
    feature_rows = tokens_t.shape[0]
    width = w_in.shape[3]
    live_mask = (slot_ids >= 0).astype(tokens_t.dtype)
    row_index = jnp.maximum(slot_ids, 0)
    slot_total = slot_ids.shape[0]
    res_in = w_in[0].reshape(-1, width)
    root_index = hot_owner[0] % lax.axis_size("dp")
    hot_pair = (from_root(w_in, "dp", root_index), from_root(w_out, "dp", root_index))
    hot_in = hot_pair[0][0].reshape(-1, width)
    hot_out_full = hot_pair[1]
    empty_sum = jnp.zeros((res_in.shape[0], slot_total), jnp.float32)
    outgoing = jnp.take(tokens_t, row_index, axis=1) * live_mask[None, :]
    incoming = lax.all_to_all(outgoing, "dp", split_axis=1, concat_axis=1, tiled=True)
    shard_rows = lax.all_gather(incoming, "expert", axis=0, tiled=True)

    def up_add_block(j, running):
        block_cols = lax.dynamic_slice_in_dim(shard_rows, j * BLOCK, BLOCK, 1)
        product = lax.cond(
            hot_flags[j] > 0,
            lambda: jnp.dot(hot_in, block_cols, preferred_element_type=jnp.float32),
            lambda: jnp.dot(res_in, block_cols, preferred_element_type=jnp.float32),
        )
        previous = lax.dynamic_slice_in_dim(running, j * BLOCK, BLOCK, 1)
        return lax.dynamic_update_slice_in_dim(running, previous + product, j * BLOCK, 1)

    gate_up = lax.fori_loop(0, num_blocks, up_add_block, empty_sum)
    half_rows = gate_up.shape[0] // 2
    hidden = (jax.nn.silu(gate_up[:half_rows]) * gate_up[half_rows:]).astype(jnp.bfloat16)
    res_moved, hot_moved = (
        lax.all_to_all(w_out, "expert", split_axis=1, concat_axis=2, tiled=True),
        lax.all_to_all(hot_out_full, "expert", split_axis=1, concat_axis=2, tiled=True),
    )
    res_by_feat = res_moved[0]
    hot_by_feat = hot_moved[0]
    start_sum = jnp.zeros((feature_rows, slot_total), jnp.float32)
    piece = lax.all_gather(hidden, "expert", axis=0, tiled=True)
    count_rows = piece.shape[0]
    groups = count_rows // half_rows
    fold_res_cols = res_by_feat.reshape(feature_rows, groups, half_rows)
    fold_hot_cols = hot_by_feat.reshape(feature_rows, groups, half_rows)

    def fold_add_block(j, running):
        hidden_block = lax.dynamic_slice_in_dim(piece, j * BLOCK, BLOCK, 1).reshape(
            groups, half_rows, BLOCK
        )
        sums = lax.cond(
            hot_flags[j] > 0,
            lambda: jnp.einsum(
                "dgf,gfb->gdb", fold_hot_cols, hidden_block, preferred_element_type=jnp.float32
            ),
            lambda: jnp.einsum(
                "dgf,gfb->gdb", fold_res_cols, hidden_block, preferred_element_type=jnp.float32
            ),
        )
        rounded = jnp.sum(sums.astype(jnp.bfloat16).astype(jnp.float32), axis=0)
        previous = lax.dynamic_slice_in_dim(running, j * BLOCK, BLOCK, 1)
        return lax.dynamic_update_slice_in_dim(running, previous + rounded, j * BLOCK, 1)

    summed = lax.fori_loop(0, num_blocks, fold_add_block, start_sum)
    expert_out = summed.astype(jnp.bfloat16)
    returned = lax.all_to_all(expert_out, "dp", split_axis=1, concat_axis=1, tiled=True)
    choose = (slot_ids[:, None] == jnp.arange(tok_local, dtype=jnp.int32)[None, :]).astype(
        jnp.float32
    )
    choose = choose * slot_weights[:, None]
    choose_high = choose.astype(jnp.bfloat16)
    choose_low = (choose - choose_high.astype(jnp.float32)).astype(jnp.bfloat16)
    mixed = jnp.dot(returned, choose_high, preferred_element_type=jnp.float32)
    mixed = mixed + jnp.dot(returned, choose_low, preferred_element_type=jnp.float32)
    return mixed.astype(jnp.bfloat16)


def solution(mesh):
    return jax.shard_map(
        local,
        mesh=mesh,
        in_specs=(
            P("expert", "dp"),
            P("dp", None),
            P("dp", None),
            P("dp", None),
            P(),
            P("dp", None, "expert", None),
            P("dp", None, "expert"),
        ),
        out_specs=P("expert", "dp"),
        check_vma=False,
    )
```

profile of v0, /device:TPU:0, one launch (start us, length us, event | category | flops | bytes accessed | tf_op | source)
XLA Modules:
  0.0 689.5 jit_solution(4974403470930709530)
XLA Ops:
  8.1 11.9 %fusion.13 = (bf16[1,7168,256]{2,0,1:T(2,128)(2,1)}, bf16[1,7168,256]{2,0,1:T(2,128)(2,1)}) fusion(bf16[1,7168,256]{2,1,0:T(8,128)(2,1)} %param.21, pred[]{:T(512)S(6)} %eq.10), kind=kLoop, calls=%fused_computation.31 | loop fusion | flops 1835008 | bytes 11010049 | tf_op args[6]
  29.1 47.0 %all_to_all.51 = bf16[896,4,256]{0,2,1:T(8,128)(2,1)S(1)} all-to-all(bf16[896,4,256]{0,2,1:T(8,128)(2,1)S(1)} %select_multiply_fusion), channel_id=1, replica_groups=mesh['expert'=8,'dp'=4] {'dp'}, dimensions={1} | all-to-all | bytes 3670016 | tf_op jit(solution)/shard_map/all_to_all | solution.py:32
  79.1 38.4 %reduce.4 = bf16[7168,256]{1,0:T(8,128)(2,1)} reduce(bf16[7168,1,256]{2,1,0:T(2,128)(2,1)} %bitcast.54, bf16[]{:T(256)} %broadcast.60), dimensions={1}, to_apply=%bitcast.26.reduce_sub_computation | reduce | bytes 7340034
  117.5 6.8 reshape.71
  124.3 5.9 all-to-all-start.1
  130.4 170.1 %all-reduce.3.cloned.1.call-done = (bf16[512,7168]{1,0:T(8,128)(2,1)}, bf16[1,7168,256]{2,0,1:T(2,128)(2,1)}) async-done(((bf16[512,7168]{1,0:T(8,128)(2,1)}, bf16[1,7168,256]{2,0,1:T(2,128)(2,1)}), (bf16[512,7168]{1,0:T(8,128)(2,1)}, bf16[1,7168,256]{2,0,1:T(2,128)(2,1)})) %all-reduce.3.cloned.1.call-update) | async-done | bytes 11010064 | tf_op jit(solution)/shard_map/psum | solution.py:11
  300.6 49.0 %all-gather.3.cloned.1.call-done = bf16[7168,1024]{1,0:T(8,128)(2,1)} async-done(((bf16[896,1024]{1,0:T(8,128)(2,1)}), bf16[7168,1024]{1,0:T(8,128)(2,1)}) %all-gather.3.cloned.1.call-update) | async-done | bytes 14680080 | tf_op jit(solution)/shard_map/all_gather | solution.py:33
  349.8 65.3 %while.26 = (s32[]{:T(128)}, f32[512,1024]{1,0:T(8,128)S(1)}, s32[8]{0:T(128)S(1)}, bf16[7168,1024]{1,0:T(8,128)(2,1)}, bf16[512,7168]{1,0:T(8,128)(2,1)}, /*ind...) while((s32[]{:T(128)}, f32[512,1024]{1,0:T(8,128)S(1)}, ...), condition=%wide.region_4.5_spmd, body=%wide.region_1.4_spmd.sunk | while | flops 939589632 | bytes 13893861 | solution.py:45
  352.7 5.2 conditional.4
  352.7 5.2 fusion.14
  360.8 5.2 conditional.4
  360.9 5.2 fusion.15
  369.0 5.2 conditional.4
  369.0 5.2 fusion.14
  377.2 5.2 conditional.4
  377.2 5.2 fusion.15
  385.3 5.2 conditional.4
  385.4 5.2 fusion.14
  393.5 5.2 conditional.4
  393.5 5.2 fusion.14
  401.7 5.2 conditional.4
  409.8 5.2 conditional.4
  409.8 5.2 fusion.14
  416.2 38.3 %reduce.5 = bf16[7168,256]{1,0:T(8,128)(2,1)} reduce(bf16[7168,1,256]{2,1,0:T(2,128)(2,1)} %bitcast.60, bf16[]{:T(256)} %broadcast.60), dimensions={1}, to_apply=%bitcast.28.reduce_sub_computation | reduce | bytes 7340034
  454.5 6.7 reshape.73
  465.9 8.3 %reshape.72 = bf16[7168,1,256]{2,1,0:T(2,128)(2,1)} reshape(bf16[8,2,114688]{2,1,0:T(2,128)(2,1)} %all-to-all-done.1) | data formatting | bytes 7340032
  474.2 5.6 copy.25
  479.8 83.8 %all-to-all-done.2 = bf16[8,2,114688]{2,1,0:T(2,128)(2,1)} async-done(((bf16[8,2,114688]{2,1,0:T(2,128)(2,1)}), bf16[8,2,114688]{2,1,0:T(2,128)(2,1)}, u32[]{:S(2)}, u32[]{:S(2)}) %all-to-all-start.2) | async-done | bytes 3670048 | tf_op jit(solution)/shard_map/all_to_all | solution.py:50
  563.6 8.3 %reshape.74 = bf16[7168,1,256]{2,1,0:T(2,128)(2,1)} reshape(bf16[8,2,114688]{2,1,0:T(2,128)(2,1)} %all-to-all-done.2) | data formatting | bytes 7340032
  571.8 5.5 copy.26
  579.4 64.8 %while.27 = (s32[]{:T(128)}, f32[896,1024]{0,1:T(8,128)}, s32[8]{0:T(128)S(1)}, bf16[2048,1024]{1,0:T(8,128)(2,1)}, bf16[896,8,256]{2,0,1:T(8,128)(2,1)}, /*inde...) while((s32[]{:T(128)}, f32[896,1024]{0,1:T(8,128)}, ...), condition=%wide.region_10.11_spmd, body=%wide.region_6.10_spmd.sunk | while | flops 471597056 | bytes 14418153 | solution.py:78
  650.4 26.1 %all_to_all.52 = bf16[896,4,256]{2,0,1:T(8,128)(2,1)} all-to-all(bf16[896,4,256]{2,0,1:T(8,128)(2,1)S(1)} %copy.19), channel_id=1, replica_groups=mesh['expert'=8,'dp'=4] {'dp'}, dimensions={1} | all-to-all | bytes 3670016 | tf_op jit(solution)/shard_map/all_to_all | solution.py:80
  (144 shorter events, 140.4 us)
Async XLA Ops:
  7.4 293.2 %all-reduce.3.cloned.1.call-start = ((), (), s32[]{:S(2)}) async-start(), calls=%async_computation.6 | async-start | bytes 29360128 | tf_op jit(solution)/shard_map/psum | solution.py:11
  8.0 11.9 %copy-start = (bf16[1,2,256,7168]{3,2,1,0:T(8,128)(2,1)S(1)}, bf16[1,2,256,7168]{3,2,1,0:T(8,128)(2,1)}, u32[]{:S(2)}) copy-start(bf16[1,2,256,7168]{3,2,1,0:T(8,128)(2,1)} %param.20) | copy-start | bytes 22020100
  23.4 0.9 copy-start.1
  23.4 1.1 copy-start.2
  23.4 326.1 %all-gather.3.cloned.1.call-start = ((), (), s32[]{:S(2)}) async-start(), calls=%async_computation.4 | async-start | bytes 16515072 | tf_op jit(solution)/shard_map/all_gather | solution.py:33
  124.2 225.5 %copy-start.4 = (s32[1,8]{1,0:T(1,128)S(1)}, s32[1,8]{1,0:T(1,128)}, u32[]{:S(2)}) copy-start(s32[1,8]{1,0:T(1,128)} %param.18) | copy-start | bytes 100
  124.3 337.0 %all-to-all-start.1 = ((bf16[8,2,114688]{2,1,0:T(2,128)(2,1)}), bf16[8,2,114688]{2,1,0:T(2,128)(2,1)}, u32[]{:S(2)}, u32[]{:S(2)}) async-start(bf16[8,2,114688]{2,1,0:T(2,128)(2,1)} %reshape.71), calls=%async_computation.1 | async-start | bytes 7340032 | tf_op jit(solution)/shard_map/all_to_all | solution.py:49
  130.2 447.1 %all-gather.5.cloned.1.call-start = ((), (), s32[]{:S(2)}) async-start(), calls=%async_computation.5 | async-start | bytes 4718592 | tf_op jit(solution)/shard_map/all_gather | solution.py:55
  461.2 102.3 %all-to-all-start.2 = ((bf16[8,2,114688]{2,1,0:T(2,128)(2,1)}), bf16[8,2,114688]{2,1,0:T(2,128)(2,1)}, u32[]{:S(2)}, u32[]{:S(2)}) async-start(bf16[8,2,114688]{2,1,0:T(2,128)(2,1)} %reshape.73), calls=%async_computation.2 | async-start | bytes 7340032 | tf_op jit(solution)/shard_map/all_to_all | solution.py:50
  650.4 28.9 %copy-start.3 = (f32[1,1024]{1,0:T(1,128)S(1)}, f32[1,1024]{1,0:T(1,128)}, u32[]{:S(2)}) copy-start(f32[1,1024]{1,0:T(1,128)} %param.17) | copy-start | bytes 12292
Sparse Core Ops, SparseCore 0:
  23.6 276.9 all-reduce.2
Sparse Core Ops, SparseCore 1:
  78.6 270.8 all-gather.2
  416.3 97.5 all-gather.4
where the time goes:
time: 692 us; the launch traced here: 689 us
  waiting for transfers between devices  303 us (44%)
  local copies, waits for them, and re-layouts  106 us (15%)
  other arithmetic  100 us (14%)
  blocking collectives  73 us (11%)
  matrix products  69.2 us (10%)
  between operations  15.7 us (2%)
  loops' own time  11.2 us (2%)
  starting transfers between devices  10.9 us (2%)
    psum x1, waiting for transfers between devices, from_root(): return lax.psum(kept, axis)  170 us
    unnamed x3, other arithmetic  88.7 us
    all_to_all x1, waiting for transfers between devices, local(): lax.all_to_all(hot_out_full, 'expert', split_axis=1, concat_axis=2, tiled...  83.8 us
    all_gather x1, waiting for transfers between devices, local(): shard_rows = lax.all_gather(incoming, 'expert', axis=0, tiled=True)  49 us
    all_to_all x1, blocking collectives, local(): lax.all_to_all(outgoing, 'dp', split_axis=1, concat_axis=1, tiled=True)  47 us
    unnamed x18, local copies, waits for them, and re-layouts  42.6 us
    all_to_all x1, blocking collectives, local(): lax.all_to_all(expert_out, 'dp', split_axis=1, concat_axis=1, tiled=True)  26.1 us
    dot_general x5, matrix products, up_add_block(): jnp.dot(res_in, block_cols, preferred_element_type=jnp.float32)  25.8 us
  transfers between devices with their start and end apart: 5, of which 3 were waited for; matrix products, arithmetic and copies ran while one was open for 27% of the time, Pallas kernels for 0%

commit v1 on v0

--- a/solution.py
+++ b/solution.py
@@ -4,6 +4,19 @@
 from jax.sharding import PartitionSpec as P
 
 BLOCK = 128
+
+
+def collect(x, axis, dim):
+    ways = lax.axis_size(axis)
+    up = [(d, (d + 1) % ways) for d in range(ways)]
+    down = [(d, (d - 1) % ways) for d in range(ways)]
+    earlier, later = ([x], [x])
+    for _ in range(ways // 2):
+        earlier.append(lax.ppermute(earlier[-1], axis, up))
+    for _ in range((ways - 1) // 2):
+        later.append(lax.ppermute(later[-1], axis, down))
+    line = jnp.concatenate([*earlier[::-1], *later[1:]], axis=dim)
+    return jnp.roll(line, (lax.axis_index(axis) - ways // 2) * x.shape[dim], axis=dim)
 
 
 def from_root(value, axis, source):
@@ -30,7 +43,7 @@
     empty_sum = jnp.zeros((res_in.shape[0], slot_total), jnp.float32)
     outgoing = jnp.take(tokens_t, row_index, axis=1) * live_mask[None, :]
     incoming = lax.all_to_all(outgoing, "dp", split_axis=1, concat_axis=1, tiled=True)
-    shard_rows = lax.all_gather(incoming, "expert", axis=0, tiled=True)
+    shard_rows = collect(incoming, "expert", 0)
 
     def up_add_block(j, running):
         block_cols = lax.dynamic_slice_in_dim(shard_rows, j * BLOCK, BLOCK, 1)

time: 692 us -> 851 us (1.23)
  starting transfers between devices: 10.9 us -> 89.1 us
  waiting for transfers between devices: 303 us -> 372 us
  local copies, waits for them, and re-layouts: 106 us -> 138 us
  blocking collectives: 73 us -> 53.1 us
    ppermute x0 -> x7, waiting for transfers between devices: none -> 153 us  [the longest x4 153 us: collect(): earlier.append(lax.ppermute(earlier[-1], axis, up))]
    ppermute x0 -> x7, starting transfers between devices: none -> 78.9 us  [the longest x3 71.8 us: collect(): later.append(lax.ppermute(later[-1], axis, down))]
    all_gather x1 -> x0, waiting for transfers between devices: 49 us -> none  [local(): shard_rows = lax.all_gather(incoming, 'expert', axis=0, tiled=True)]
    psum x1, waiting for transfers between devices: 170 us -> 134 us  [from_root(): return lax.psum(kept, axis)]
    unnamed x18 -> x29, local copies, waits for them, and re-layouts: 42.6 us -> 64.6 us
    all_to_all x1, blocking collectives: 47 us -> 27 us  [local(): lax.all_to_all(outgoing, 'dp', split_axis=1, concat_axis=1, tiled=True)]
  transfers between devices with their start and end apart: 5 -> 11, of which waited for: 3 -> 5; matrix products, arithmetic and copies ran while one was open for 27% -> 27% of each run, Pallas kernels for 0% -> 0%
where the time goes in v1:
time: 851 us; the launch traced here: 847 us
  waiting for transfers between devices  372 us (44%)
  local copies, waits for them, and re-layouts  138 us (16%)
  other arithmetic  102 us (12%)
  starting transfers between devices  89.1 us (10%)
  matrix products  69.2 us (8%)
  blocking collectives  53.1 us (6%)
  between operations  14.3 us (2%)
  loops' own time  9.98 us (1%)
    ppermute x4, waiting for transfers between devices, collect(): earlier.append(lax.ppermute(earlier[-1], axis, up))  153 us
    psum x1, waiting for transfers between devices, from_root(): return lax.psum(kept, axis)  134 us
    unnamed x3, other arithmetic  88.5 us
    all_to_all x1, waiting for transfers between devices, local(): lax.all_to_all(hot_out_full, 'expert', split_axis=1, concat_axis=2, tiled...  85.1 us
    ppermute x3, starting transfers between devices, collect(): later.append(lax.ppermute(later[-1], axis, down))  71.8 us
    unnamed x29, local copies, waits for them, and re-layouts  64.6 us
    all_to_all x1, blocking collectives, local(): lax.all_to_all(outgoing, 'dp', split_axis=1, concat_axis=1, tiled=True)  27 us
    all_to_all x1, blocking collectives, local(): lax.all_to_all(expert_out, 'dp', split_axis=1, concat_axis=1, tiled=True)  26.1 us
  transfers between devices with their start and end apart: 11, of which 5 were waited for; matrix products, arithmetic and copies ran while one was open for 27% of the time, Pallas kernels for 0%

profile of v1, /device:TPU:0, one launch (start us, length us, event | category | flops | bytes accessed | tf_op | source)
XLA Modules:
  0.0 847.4 jit_solution(7725136745419476184)
XLA Ops:
  14.2 27.0 %all_to_all.51 = bf16[896,4,256]{0,2,1:T(8,128)(2,1)} all-to-all(bf16[896,4,256]{0,2,1:T(8,128)(2,1)S(1)} %select_multiply_fusion), channel_id=1, replica_groups=mesh['expert'=8,'dp'=4] {'dp'}, dimensions={1} | all-to-all | bytes 3670016 | tf_op jit(solution)/shard_map/all_to_all | solution.py:45
  46.3 42.8 %collective-permute-done = bf16[896,1024]{1,0:T(8,128)(2,1)} collective-permute-done((bf16[896,1024]{1,0:T(8,128)(2,1)S(1)}, bf16[896,1024]{1,0:T(8,128)(2,1)}, u32[]{:S(2)}, u32[]{:S(2)}) %collective-permute-start) | collective-permute-done | bytes 1835040 | tf_op jit(solution)/shard_map/ppermute | solution.py:15
  94.5 72.8 %collective-permute-done.1 = bf16[896,1024]{1,0:T(8,128)(2,1)} collective-permute-done((bf16[896,1024]{1,0:T(8,128)(2,1)}, bf16[896,1024]{1,0:T(8,128)(2,1)}, u32[]{:S(2)}, u32[]{:S(2)}) %collective-permute-start.1) | collective-permute-done | bytes 1835040 | tf_op jit(solution)/shard_map/ppermute | solution.py:15
  169.8 11.8 %fusion.13 = (bf16[1,7168,256]{2,0,1:T(2,128)(2,1)}, bf16[1,7168,256]{2,0,1:T(2,128)(2,1)}) fusion(bf16[1,7168,256]{2,1,0:T(8,128)(2,1)} %param.21, pred[]{:T(512)S(6)} %eq.22), kind=kLoop, calls=%fused_computation.48 | loop fusion | flops 1835008 | bytes 11010049 | tf_op args[6]
  181.6 28.4 %collective-permute-start.5 = (bf16[896,1024]{1,0:T(8,128)(2,1)}, bf16[896,1024]{1,0:T(8,128)(2,1)}, u32[]{:S(2)}, u32[]{:S(2)}) collective-permute-start(bf16[896,1024]{1,0:T(8,128)(2,1)} %collective-permute-done.4), channel_id=1, source_target_pairs={{0,28},{4,0},{8,4},{12,8},{16,12},{20,16},{24,20},{28,24},{1,29},{... | collective-permute-start | bytes 5505032 | tf_op jit(solution)/shard_map/ppermute | solution.py:17
  210.0 37.2 %collective-permute-done.2 = bf16[896,1024]{1,0:T(8,128)(2,1)} collective-permute-done((bf16[896,1024]{1,0:T(8,128)(2,1)}, bf16[896,1024]{1,0:T(8,128)(2,1)}, u32[]{:S(2)}, u32[]{:S(2)}) %collective-permute-start.2) | collective-permute-done | bytes 1835040 | tf_op jit(solution)/shard_map/ppermute | solution.py:15
  253.1 38.6 %collective-permute-start.6 = (bf16[896,1024]{1,0:T(8,128)(2,1)}, bf16[896,1024]{1,0:T(8,128)(2,1)}, u32[]{:S(2)}, u32[]{:S(2)}) collective-permute-start(bf16[896,1024]{1,0:T(8,128)(2,1)} %collective-permute-done.5), channel_id=1, source_target_pairs={{0,28},{4,0},{8,4},{12,8},{16,12},{20,16},{24,20},{28,24},{1,29},{... | collective-permute-start | bytes 5505032 | tf_op jit(solution)/shard_map/ppermute | solution.py:17
  292.2 38.3 %reduce.4 = bf16[7168,256]{1,0:T(8,128)(2,1)} reduce(bf16[7168,1,256]{2,1,0:T(2,128)(2,1)} %bitcast.54, bf16[]{:T(256)} %broadcast.60), dimensions={1}, to_apply=%bitcast.26.reduce_sub_computation | reduce | bytes 7340034
  330.6 6.7 reshape.71
  365.7 7.8 constant_dynamic-slice_fusion.3
  373.6 133.7 %all-reduce.3.cloned.1.call-done = (bf16[512,7168]{1,0:T(8,128)(2,1)}, bf16[1,7168,256]{2,0,1:T(2,128)(2,1)}) async-done(((bf16[512,7168]{1,0:T(8,128)(2,1)}, bf16[1,7168,256]{2,0,1:T(2,128)(2,1)}), (bf16[512,7168]{1,0:T(8,128)(2,1)}, bf16[1,7168,256]{2,0,1:T(2,128)(2,1)})) %all-reduce.3.cloned.1.call-update) | async-done | bytes 11010064 | tf_op jit(solution)/shard_map/psum | solution.py:24
  507.5 64.5 %while.26 = (s32[]{:T(128)}, f32[512,1024]{1,0:T(8,128)S(1)}, s32[8]{0:T(128)S(1)}, bf16[7168,1024]{1,0:T(8,128)(2,1)}, bf16[512,7168]{1,0:T(8,128)(2,1)}, /*ind...) while((s32[]{:T(128)}, f32[512,1024]{1,0:T(8,128)S(1)}, ...), condition=%wide.region_4.5_spmd, body=%wide.region_1.4_spmd.sunk | while | flops 939589632 | bytes 13893861 | solution.py:58
  510.3 5.2 conditional.4
  510.3 5.2 fusion.14
  518.4 5.2 conditional.4
  526.4 5.2 conditional.4
  534.5 5.2 conditional.4
  542.6 5.2 conditional.4
  542.6 5.2 fusion.14
  550.6 5.2 conditional.4
  558.7 5.2 conditional.4
  566.8 5.2 conditional.4
  573.2 38.4 %reduce.5 = bf16[7168,256]{1,0:T(8,128)(2,1)} reduce(bf16[7168,1,256]{2,1,0:T(2,128)(2,1)} %bitcast.60, bf16[]{:T(256)} %broadcast.60), dimensions={1}, to_apply=%bitcast.28.reduce_sub_computation | reduce | bytes 7340034
  611.6 6.7 reshape.73
  618.3 5.5 all-to-all-start.2
  623.8 8.3 reshape.72
  632.0 5.5 copy.25
  637.5 85.1 %all-to-all-done.2 = bf16[8,2,114688]{2,1,0:T(2,128)(2,1)} async-done(((bf16[8,2,114688]{2,1,0:T(2,128)(2,1)}), bf16[8,2,114688]{2,1,0:T(2,128)(2,1)}, u32[]{:S(2)}, u32[]{:S(2)}) %all-to-all-start.2) | async-done | bytes 3670048 | tf_op jit(solution)/shard_map/all_to_all | solution.py:63
  722.6 8.2 reshape.74
  730.9 5.6 copy.26
  738.6 64.0 %while.27 = (s32[]{:T(128)}, f32[896,1024]{0,1:T(8,128)}, s32[8]{0:T(128)S(1)}, bf16[2048,1024]{1,0:T(8,128)(2,1)}, bf16[896,8,256]{2,0,1:T(8,128)(2,1)}, /*inde...) while((s32[]{:T(128)}, f32[896,1024]{0,1:T(8,128)}, ...), condition=%wide.region_10.11_spmd, body=%wide.region_6.10_spmd.sunk | while | flops 471597056 | bytes 14418153 | solution.py:91
  808.9 26.1 %all_to_all.52 = bf16[896,4,256]{2,0,1:T(8,128)(2,1)} all-to-all(bf16[896,4,256]{2,0,1:T(8,128)(2,1)S(1)} %copy.19), channel_id=1, replica_groups=mesh['expert'=8,'dp'=4] {'dp'}, dimensions={1} | all-to-all | bytes 3670016 | tf_op jit(solution)/shard_map/all_to_all | solution.py:93
  (168 shorter events, 203.6 us)
Async XLA Ops:
  6.5 500.7 %all-reduce.3.cloned.1.call-start = ((), (), s32[]{:S(2)}) async-start(), calls=%async_computation.5 | async-start | bytes 29360128 | tf_op jit(solution)/shard_map/psum | solution.py:24
  44.1 44.9 %collective-permute-start = (bf16[896,1024]{1,0:T(8,128)(2,1)S(1)}, bf16[896,1024]{1,0:T(8,128)(2,1)}, u32[]{:S(2)}, u32[]{:S(2)}) collective-permute-start(bf16[896,1024]{1,0:T(8,128)(2,1)S(1)} %copy.21), channel_id=1, source_target_pairs={{0,4},{4,8},{8,12},{12,16},{16,20},{20,24},{24,28},{28,0},{1,5},{5... | collective-permute-start | bytes 5505032 | tf_op jit(solution)/shard_map/ppermute | solution.py:15
  89.0 78.3 %collective-permute-start.1 = (bf16[896,1024]{1,0:T(8,128)(2,1)}, bf16[896,1024]{1,0:T(8,128)(2,1)}, u32[]{:S(2)}, u32[]{:S(2)}) collective-permute-start(bf16[896,1024]{1,0:T(8,128)(2,1)} %collective-permute-done), channel_id=1, source_target_pairs={{0,4},{4,8},{8,12},{12,16},{16,20},{20,24},{24,28},{28,0},{1,5},{5... | collective-permute-start | bytes 5505032 | tf_op jit(solution)/shard_map/ppermute | solution.py:15
  89.7 91.8 %collective-permute-start.4 = (bf16[896,1024]{1,0:T(8,128)(2,1)S(1)}, bf16[896,1024]{1,0:T(8,128)(2,1)}, u32[]{:S(2)}, u32[]{:S(2)}) collective-permute-start(bf16[896,1024]{1,0:T(8,128)(2,1)S(1)} %copy.21), channel_id=1, source_target_pairs={{0,28},{4,0},{8,4},{12,8},{16,12},{20,16},{24,20},{28,24},{1,29},{... | collective-permute-start | bytes 5505032 | tf_op jit(solution)/shard_map/ppermute | solution.py:17
  167.3 79.9 %collective-permute-start.2 = (bf16[896,1024]{1,0:T(8,128)(2,1)}, bf16[896,1024]{1,0:T(8,128)(2,1)}, u32[]{:S(2)}, u32[]{:S(2)}) collective-permute-start(bf16[896,1024]{1,0:T(8,128)(2,1)} %collective-permute-done.1), channel_id=1, source_target_pairs={{0,4},{4,8},{8,12},{12,16},{16,20},{20,24},{24,28},{28,0},{1,5},{5... | collective-permute-start | bytes 5505032 | tf_op jit(solution)/shard_map/ppermute | solution.py:15
  181.6 71.5 %collective-permute-start.5 = (bf16[896,1024]{1,0:T(8,128)(2,1)}, bf16[896,1024]{1,0:T(8,128)(2,1)}, u32[]{:S(2)}, u32[]{:S(2)}) collective-permute-start(bf16[896,1024]{1,0:T(8,128)(2,1)} %collective-permute-done.4), channel_id=1, source_target_pairs={{0,28},{4,0},{8,4},{12,8},{16,12},{20,16},{24,20},{28,24},{1,29},{... | collective-permute-start | bytes 5505032 | tf_op jit(solution)/shard_map/ppermute | solution.py:17
  247.2 94.9 %collective-permute-start.3 = (bf16[896,1024]{1,0:T(8,128)(2,1)}, bf16[896,1024]{1,0:T(8,128)(2,1)}, u32[]{:S(2)}, u32[]{:S(2)}) collective-permute-start(bf16[896,1024]{1,0:T(8,128)(2,1)} %collective-permute-done.2), channel_id=1, source_target_pairs={{0,4},{4,8},{8,12},{12,16},{16,20},{20,24},{24,28},{28,0},{1,5},{5... | collective-permute-start | bytes 5505032 | tf_op jit(solution)/shard_map/ppermute | solution.py:15
  253.1 99.2 %collective-permute-start.6 = (bf16[896,1024]{1,0:T(8,128)(2,1)}, bf16[896,1024]{1,0:T(8,128)(2,1)}, u32[]{:S(2)}, u32[]{:S(2)}) collective-permute-start(bf16[896,1024]{1,0:T(8,128)(2,1)} %collective-permute-done.5), channel_id=1, source_target_pairs={{0,28},{4,0},{8,4},{12,8},{16,12},{20,16},{24,20},{28,24},{1,29},{... | collective-permute-start | bytes 5505032 | tf_op jit(solution)/shard_map/ppermute | solution.py:17
  337.3 281.0 %all-to-all-start.1 = ((bf16[8,2,114688]{2,1,0:T(2,128)(2,1)}), bf16[8,2,114688]{2,1,0:T(2,128)(2,1)}, u32[]{:S(2)}, u32[]{:S(2)}) async-start(bf16[8,2,114688]{2,1,0:T(2,128)(2,1)} %reshape.71), calls=%async_computation.1 | async-start | bytes 7340032 | tf_op jit(solution)/shard_map/all_to_all | solution.py:62
  341.8 394.6 %all-gather.2.cloned.1.call-start = ((), (), s32[]{:S(2)}) async-start(), calls=%async_computation.4 | async-start | bytes 4718592 | tf_op jit(solution)/shard_map/all_gather | solution.py:68
  365.7 141.8 %copy-start.2 = (s32[1,8]{1,0:T(1,128)S(1)}, s32[1,8]{1,0:T(1,128)}, u32[]{:S(2)}) copy-start(s32[1,8]{1,0:T(1,128)} %param.18) | copy-start | bytes 100
  618.3 104.3 %all-to-all-start.2 = ((bf16[8,2,114688]{2,1,0:T(2,128)(2,1)}), bf16[8,2,114688]{2,1,0:T(2,128)(2,1)}, u32[]{:S(2)}, u32[]{:S(2)}) async-start(bf16[8,2,114688]{2,1,0:T(2,128)(2,1)} %reshape.73), calls=%async_computation.2 | async-start | bytes 7340032 | tf_op jit(solution)/shard_map/all_to_all | solution.py:63
  808.9 29.0 %copy-start = (s32[1,1024]{1,0:T(1,128)S(1)}, s32[1,1024]{1,0:T(1,128)}, u32[]{:S(2)}) copy-start(s32[1,1024]{1,0:T(1,128)} %param.16) | copy-start | bytes 12292
  808.9 29.0 %copy-start.1 = (f32[1,1024]{1,0:T(1,128)S(1)}, f32[1,1024]{1,0:T(1,128)}, u32[]{:S(2)}) copy-start(f32[1,1024]{1,0:T(1,128)} %param.17) | copy-start | bytes 12292
Sparse Core Ops, SparseCore 0:
  253.2 254.0 all-reduce.2
  573.3 99.5 all-gather.1
